TPU v7x, 256 devices: a whole 4x4x8 slice. The times are simulated.
256 devices in a mesh: sub: 16 (over y, z_lo, core), mem: 16 (over x, z_hi).
Axes of the slice: x: 4, y: 4, z: 8 (z_hi: 4, z_lo: 2; z = z_hi * 2 + z_lo), core: 2. Of those that a mesh axis runs over, the one named last changes fastest.
Arguments:
- now_field: float32 [128, 1024, 512], P('mem', 'sub'), may hold values from -6 to 6
- prev_field: float32 [128, 1024, 512], P('mem', 'sub'), may hold values from -6 to 6
- speed: float32 [1024, 512], P('sub'), may hold values from 0.05 to 0.45
- obs_cells: int32 [2048], P('sub'), may hold values from 0 to 32767
- obs_values: float32 [2048], replicated, may hold values from -6 to 6
- obs_precision: float32 [2048], replicated, may hold values from 0.1 to 1
- taper: float32 [2048, 2048], P(('sub', 'mem')), may hold values from 0.05 to 1
Outputs:
- now_analysis: float32 [128, 1024, 512], P('mem', 'sub')
- prev_analysis: float32 [128, 1024, 512], P('mem', 'sub')
Inputs may be any that keep to these rules, and one draw needn't show every extreme that they name: `obs_cells`: entry o is a cell of subdomain o // 128, counted row by row within that subdomain's 64 x 512 cells.
All inputs are finite; a program needn't handle non-finite values.
Results may differ from a plain program's by a relative error of at most 0.00019.
Values sent between devices are 32-bit elements; how exact they have to be, the bound alone decides.
A program may use at most 64 MiB of HBM per device.

v0:
```python
import functools
import math

import jax
import jax.numpy as jnp
from jax import lax
from jax.experimental import pallas as pl
from jax.experimental.pallas import tpu as pltpu
from jax.sharding import PartitionSpec as P

ENS = 128
STEPS = 8
NS_ITERS = 8
BLOCK = 256
GROUP = 16
OWN = 8
ROWS = 64
STRIP = 4
COLS = 512
OBS_SUB = 128
TALL = ROWS + 2 * STEPS
MESH = pl.DeviceIdType.MESH
F32 = jnp.float32


def halves(x):
    high = x.astype(jnp.bfloat16)
    low = (x - high.astype(F32)).astype(jnp.bfloat16)
    return high, low


def side(x):
    return jnp.concatenate(halves(x), axis=1)


def tile(x):
    both = side(x)
    return jnp.concatenate([both, both], axis=0)


def product(left, right):
    wide = jnp.dot(left, right, preferred_element_type=F32)
    width = wide.shape[1] // 2
    return wide[:, :width] + wide[:, width:]


def forecast_rows(field, pace, step, low, high, unroll):
    source, target = (step + 1) % 2, step % 2
    lane = lax.broadcasted_iota(jnp.int32, (OWN, COLS), 1)

    def one(row, held):
        above, here = held
        below = field[source, row + 1]
        west = jnp.where(lane == 0, 0.0, pltpu.roll(here, 1, 1))
        east = jnp.where(lane == COLS - 1, 0.0, pltpu.roll(here, COLS - 1, 1))
        spread = below + above + east + west - 4.0 * here
        field[target, row] = 2.0 * here - field[target, row] + pace[row] * spread
        return here, below

    lax.fori_loop(low, high, one, (field[source, low - 1], field[source, low]), unroll=unroll)


def kernel(
    now_hbm,
    prev_hbm,
    speed_hbm,
    cells_ref,
    values_ref,
    precision_ref,
    taper_ref,
    now_out,
    prev_out,
    raw,
    rim,
    pace_raw,
    pace_rim,
    pace,
    field,
    seen,
    gram,
    iterate,
    root,
    arrived,
    leaving,
    settled,
    load_sem,
    rim_send,
    rim_recv,
    obs_send,
    obs_recv,
    out_send,
    out_recv,
    back_send,
    back_recv,
):
    mem, sub = lax.axis_index("mem"), lax.axis_index("sub")
    core = lax.rem(sub, 2)
    near = lax.rem(lax.div(sub, 2), 2)
    tier = lax.div(sub, 4)
    above = lax.rem(sub + GROUP - 1, GROUP)
    below = lax.rem(sub + 1, GROUP)
    twin = sub + 1 - 2 * core
    across = sub + 2 - 4 * near
    tiers = [lax.rem(sub + 4 * k, GROUP) for k in (1, 2, 3)]

    barrier = pltpu.get_barrier_semaphore()
    for other in (above, below, twin, across, *tiers):
        pl.semaphore_signal(barrier, inc=1, device_id={"sub": other}, device_id_type=MESH)

    def greet(step, _):
        pl.semaphore_signal(
            barrier, inc=1, device_id={"mem": lax.rem(mem + step, GROUP)}, device_id_type=MESH
        )
        return 0

    lax.fori_loop(1, GROUP, greet, 0)

    loads = [
        pltpu.make_async_copy(now_hbm, raw.at[0], load_sem.at[0]),
        pltpu.make_async_copy(prev_hbm, raw.at[1], load_sem.at[1]),
        pltpu.make_async_copy(speed_hbm, pace_raw, load_sem.at[2]),
    ]
    for load in loads:
        load.start()
    for load in loads:
        load.wait()

    pl.semaphore_wait(barrier, GROUP - 1 + 7)

    rims = []
    for side_index, (other, first) in enumerate(((below, ROWS - STEPS), (above, 0))):
        for index, source in enumerate((raw.at[0], raw.at[1])):
            rims.append(
                pltpu.make_async_remote_copy(
                    src_ref=source.at[:, first : first + STEPS, :],
                    dst_ref=rim.at[side_index, index],
                    send_sem=rim_send.at[side_index, index],
                    recv_sem=rim_recv.at[side_index, index],
                    device_id={"sub": other},
                    device_id_type=MESH,
                )
            )
        rims.append(
            pltpu.make_async_remote_copy(
                src_ref=pace_raw.at[first : first + STEPS, :],
                dst_ref=pace_rim.at[side_index],
                send_sem=rim_send.at[side_index, 2],
                recv_sem=rim_recv.at[side_index, 2],
                device_id={"sub": other},
                device_id_type=MESH,
            )
        )
    for copy in rims:
        copy.start()

    def turn(group, _):
        at = pl.multiple_of(group * 8, 8)
        for index in range(2):
            field[index, pl.ds(at + STEPS, 8)] = jnp.transpose(raw[index, :, pl.ds(at, 8), :], (1, 0, 2))
        rows = pace_raw[pl.ds(at, 8), :]
        pace[pl.ds(at + STEPS, 8)] = jnp.broadcast_to(rows[:, None, :], (8, OWN, COLS))
        return 0

    lax.fori_loop(0, ROWS // 8, turn, 0)

    for step in range(1, STEPS + 1):
        forecast_rows(field, pace, step, STEPS + step, STEPS + ROWS - step, 2)

    def ship(part, edges):
        def one(step, _):
            peer = lax.rem(mem + step, GROUP)
            outer = jnp.logical_or(peer < 2, peer > GROUP - 3)

            def go():
                pltpu.make_async_remote_copy(
                    src_ref=field.at[:, STEPS + STRIP * peer + part],
                    dst_ref=arrived.at[part, mem],
                    send_sem=out_send,
                    recv_sem=out_recv.at[part],
                    device_id={"mem": peer},
                    device_id_type=MESH,
                ).start()

            if edges is None:
                go()
            else:
                pl.when(outer if edges else jnp.logical_not(outer))(go)
            return 0

        lax.fori_loop(1, GROUP, one, 0)

    ship(0, False)

    for copy in rims:
        copy.wait_recv()
    for side_index, (at, outside) in enumerate(((0, sub == 0), (STEPS + ROWS, sub == GROUP - 1))):
        keep = jnp.where(outside, 0.0, 1.0)
        for index in range(2):
            field[index, at : at + STEPS] = jnp.transpose(rim[side_index, index], (1, 0, 2)) * keep
        rows = pace_rim[side_index] * keep
        pace[at : at + STEPS] = jnp.broadcast_to(rows[:, None, :], (STEPS, OWN, COLS))
    for step in range(1, STEPS + 1):
        forecast_rows(field, pace, step, step, STEPS + step, 2)
        forecast_rows(field, pace, step, STEPS + ROWS - step, ROWS + 2 * STEPS - step, 2)

    lane_all = lax.broadcasted_iota(jnp.int32, (OWN, COLS), 1)
    lane = lax.broadcasted_iota(jnp.int32, (OWN, OBS_SUB), 1)

    def pick(index, held):
        cell = cells_ref[index]
        row = field[0, STEPS + lax.div(cell, COLS)]
        kept = jnp.where(lane_all == lax.rem(cell, COLS), row, 0.0)
        kept = kept[:, :128] + kept[:, 128:256] + kept[:, 256:384] + kept[:, 384:]
        return jnp.where(lane == index, jnp.sum(kept, axis=1, keepdims=True), held)

    seen[core, tier, near, mem] = lax.fori_loop(
        0, OBS_SUB, pick, jnp.zeros((OWN, OBS_SUB), F32), unroll=8
    )

    def tell(step, _):
        pltpu.make_async_remote_copy(
            src_ref=seen.at[core, tier, near, mem],
            dst_ref=seen.at[core, tier, near, mem],
            send_sem=obs_send.at[0],
            recv_sem=obs_recv.at[0],
            device_id={"mem": lax.rem(mem + step, GROUP)},
            device_id_type=MESH,
        ).start()
        return 0

    lax.fori_loop(1, GROUP, tell, 0)

    ship(0, True)
    for part in range(1, STRIP):
        ship(part, None)
    for part in range(STRIP):
        arrived[part, mem] = field[:, STEPS + STRIP * mem + part]

    whole = seen.at[0, 0, 0, pl.ds(0, GROUP - 1)]
    pltpu.make_async_copy(whole, whole, obs_recv.at[0]).wait()

    def pass_on(block, other, number):
        copy = pltpu.make_async_remote_copy(
            src_ref=block,
            dst_ref=block,
            send_sem=obs_send.at[number],
            recv_sem=obs_recv.at[number],
            device_id={"sub": other},
            device_id_type=MESH,
        )
        copy.start()
        return copy

    own = seen.at[core, tier, near]
    met = seen.at[core, tier, 1 - near]
    crossing = pass_on(own, across, 1)
    for other in tiers:
        pass_on(own, other, 2)
    crossing.wait_recv()
    for other in tiers:
        pass_on(met, other, 3)
    third = seen.at[0, pl.ds(0, 3), 0]
    pltpu.make_async_copy(third, third, obs_recv.at[2]).wait()
    pltpu.make_async_copy(third, third, obs_recv.at[3]).wait()
    pass_on(seen.at[core], twin, 4).wait_recv()

    blocks = taper_ref.shape[0]
    lines = blocks * ENS
    gram[...] = jnp.zeros_like(gram)

    def gather_gram(index, _):
        lefts, rights = [], []
        for close in range(2):
            place = lax.rem(index, 4)
            sheet = lax.div(index, 4)
            observed = seen[sheet, place, close].reshape(ENS, OBS_SUB)
            mean = jnp.mean(observed, axis=0, keepdims=True)
            pert = observed - mean
            at = pl.ds(pl.multiple_of((4 * place + 2 * close + sheet) * OBS_SUB, OBS_SUB), OBS_SUB)
            weight = taper_ref[:, at] * precision_ref[:, at]
            pulling = weight * (values_ref[:, at] - mean)
            stack = [pert * weight[b : b + 1] for b in range(blocks)]
            lefts.append(side(jnp.concatenate([*stack, pulling, jnp.zeros_like(pulling)], axis=0)))
            high, low = halves(pert)
            rights.append(
                jnp.concatenate(
                    [jnp.concatenate([high, high], axis=1), jnp.concatenate([low, low], axis=1)], axis=0
                )
            )
        gram[...] += lax.dot_general(
            jnp.concatenate(lefts, axis=1),
            jnp.concatenate(rights, axis=1),
            (((1,), (1,)), ((), ())),
            preferred_element_type=F32,
        )
        return 0

    lax.fori_loop(0, GROUP // 2, gather_gram, 0)

    diagonal = lax.broadcasted_iota(jnp.int32, (ENS, ENS), 0) == lax.broadcasted_iota(
        jnp.int32, (ENS, ENS), 1
    )
    eye = jnp.where(diagonal, 1.0, 0.0)
    scales = []
    for b in range(blocks):
        wide = gram[b * ENS : (b + 1) * ENS, :]
        full = wide[:, :ENS] + wide[:, ENS:] + (ENS - 1.0) * eye
        scale = jnp.sum(jnp.sum(full * eye, axis=1, keepdims=True), axis=0, keepdims=True)
        scales.append(scale)
        iterate[b] = full / scale
        root[b] = eye

    def sweep(_, carry):
        for b in range(blocks):
            held, base = iterate[b], root[b]
            factor = 1.5 * eye - 0.5 * product(side(base), tile(held))
            iterate[b] = product(side(held), tile(factor))
            root[b] = product(side(factor), tile(base))
        return carry

    lax.fori_loop(0, NS_ITERS, sweep, 0)

    for b in range(blocks):
        final = root[b] / jnp.sqrt(scales[b])
        wide = gram[lines : lines + 8, :]
        pulled = (wide[:, :ENS] + wide[:, ENS:])[b : b + 1]
        pulled = jnp.broadcast_to(pulled, (16, ENS))
        right = tile(final)
        shift = product(side(product(side(pulled), right)), right)
        iterate[b] = math.sqrt(ENS - 1.0) * final + shift[0:1]

    def settle(part):
        for half in range(COLS // BLOCK):
            mixing = side(iterate[2 * part + half])
            cut = slice(half * BLOCK, (half + 1) * BLOCK)
            x = jnp.concatenate(
                [arrived[part, :, index, :, cut].reshape(ENS, BLOCK) for index in range(2)], axis=1
            )
            center = jnp.mean(x, axis=0, keepdims=True)
            moved = product(mixing, tile(x - center)) + center
            for index in range(2):
                leaving[part, :, index, :, cut] = moved[:, index * BLOCK : (index + 1) * BLOCK].reshape(
                    GROUP, OWN, BLOCK
                )

        def back(step, _):
            peer = lax.rem(mem + step, GROUP)
            pltpu.make_async_remote_copy(
                src_ref=leaving.at[part, peer],
                dst_ref=settled.at[:, STRIP * mem + part],
                send_sem=back_send,
                recv_sem=back_recv,
                device_id={"mem": peer},
                device_id_type=MESH,
            ).start()
            return 0

        lax.fori_loop(1, GROUP, back, 0)
        settled[:, STRIP * mem + part] = leaving[part, mem]

    for part in range(STRIP):
        strip = arrived.at[0, pl.ds(0, GROUP - 1)]
        pltpu.make_async_copy(strip, strip, out_recv.at[part]).wait()
        settle(part)

    everything = arrived.at[:, pl.ds(0, GROUP - 1)]
    pltpu.make_async_copy(everything, everything, back_recv).wait()

    def finish(group, _):
        at = pl.multiple_of(group * 8, 8)
        for index, out in enumerate((now_out, prev_out)):
            out[:, pl.ds(at, 8), :] = jnp.transpose(settled[index, pl.ds(at, 8)], (1, 0, 2))
        return 0

    lax.fori_loop(0, ROWS // 8, finish, 0)

    for copy in rims:
        copy.wait_send()
    pltpu.make_async_copy(whole, whole, obs_send.at[0]).wait()
    pltpu.make_async_copy(own, own, obs_send.at[1]).wait()
    pltpu.make_async_copy(third, third, obs_send.at[2]).wait()
    pltpu.make_async_copy(third, third, obs_send.at[3]).wait()
    pltpu.make_async_copy(seen.at[0], seen.at[0], obs_send.at[4]).wait()
    pltpu.make_async_copy(everything, everything, out_send).wait()
    pltpu.make_async_copy(everything, everything, back_send).wait()


def local(now_field, prev_field, speed, obs_cells, obs_values, obs_precision, taper):
    blocks = taper.shape[0]
    hbm = pl.BlockSpec(memory_space=pl.ANY)
    vmem = pl.BlockSpec(memory_space=pltpu.VMEM)
    outs = jax.ShapeDtypeStruct((OWN, ROWS, COLS), F32)
    return pl.pallas_call(
        kernel,
        out_shape=(outs, outs),
        in_specs=[hbm, hbm, hbm, pl.BlockSpec(memory_space=pltpu.SMEM), vmem, vmem, vmem],
        out_specs=(vmem, vmem),
        scratch_shapes=[
            pltpu.VMEM((2, OWN, ROWS, COLS), F32),
            pltpu.VMEM((2, 2, OWN, STEPS, COLS), F32),
            pltpu.VMEM((ROWS, COLS), F32),
            pltpu.VMEM((2, STEPS, COLS), F32),
            pltpu.VMEM((TALL, OWN, COLS), F32),
            pltpu.VMEM((2, TALL, OWN, COLS), F32),
            pltpu.VMEM((2, 4, 2, GROUP, OWN, OBS_SUB), F32),
            pltpu.VMEM((blocks * ENS + 16, 2 * ENS), F32),
            pltpu.VMEM((blocks, ENS, ENS), F32),
            pltpu.VMEM((blocks, ENS, ENS), F32),
            pltpu.VMEM((STRIP, GROUP, 2, OWN, COLS), F32),
            pltpu.VMEM((STRIP, GROUP, 2, OWN, COLS), F32),
            pltpu.VMEM((2, ROWS, OWN, COLS), F32),
            pltpu.SemaphoreType.DMA((3,)),
            pltpu.SemaphoreType.DMA((2, 3)),
            pltpu.SemaphoreType.DMA((2, 3)),
            pltpu.SemaphoreType.DMA((5,)),
            pltpu.SemaphoreType.DMA((5,)),
            pltpu.SemaphoreType.DMA,
            pltpu.SemaphoreType.DMA((STRIP,)),
            pltpu.SemaphoreType.DMA,
            pltpu.SemaphoreType.DMA,
        ],
        compiler_params=pltpu.CompilerParams(
            collective_id=0, has_side_effects=True, vmem_limit_bytes=48 * 2**20
        ),
    )(
        now_field,
        prev_field,
        speed,
        obs_cells,
        obs_values[None, :],
        obs_precision[None, :],
        taper,
    )


def solution(mesh):
    placed = (
        P("mem", "sub", None),
        P("mem", "sub", None),
        P("sub", None),
        P("sub"),
        P(),
        P(),
        P(("sub", "mem"), None),
    )
    return jax.shard_map(
        local,
        mesh=mesh,
        in_specs=placed,
        out_specs=(P("mem", "sub", None), P("mem", "sub", None)),
        check_vma=False,
    )
```

profile of v0, /device:TPU:1, one launch (start us, length us, event | category | flops | bytes accessed | tf_op | source)
XLA Modules:
  0.0 164.3 jit_solution(6515124847799832556)
XLA Ops:
  0.6 0.0 copy-start.6
  0.6 0.6 copy-done.6
  1.3 0.0 copy-start
  1.3 1.2 copy-done
  2.5 0.0 copy-start.1
  2.5 1.2 copy-done.1
  3.7 0.0 copy-start.2
  3.7 0.9 copy-done.2
  4.6 0.0 copy-start.3
  4.6 0.8 copy-done.3
  5.5 0.0 copy-start.4
  5.5 0.7 copy-done.4
  6.2 0.0 copy-start.5
  6.2 0.7 copy-done.5
  6.9 155.5 %shard_map.86 = (f32[8,64,512]{2,1,0:T(8,128)S(1)}, f32[8,64,512]{2,1,0:T(8,128)S(1)}) custom-call(f32[8,64,512]{2,1,0:T(8,128)S(1)} %copy-done, f32[8,64,512]{2,1,0:T(8,128)S(1)} %copy-done.1, f32[64,512]{1,0:T(8,128)S(1)} %copy-done.2, s32[128]{0:T(128)S(1)} %copy-done.6, f32[1,2048]{1,0:T(1,128)S(1)} %bitcast.2, f32[1,2048]{1,0:T(1,128)S(1)} %bitcast.3, ...), custom_call_target="tpu_custom_call" | custom-call | tf_op jit(solution)/shard_map/pallas_call | solution.py:393
  162.4 1.0 copy.11
  163.3 1.0 copy.12
Async XLA Ops:
  0.6 0.7 copy-start.6
  1.3 1.2 copy-start
  2.5 1.2 copy-start.1
  3.7 0.9 copy-start.2
  4.6 0.8 copy-start.3
  5.5 0.7 copy-start.4
  6.2 0.7 copy-start.5
where the time goes:
time: 165 us; the launch traced here: 164 us
  Pallas kernels  155 us (94%)
  local copies, waits for them, and re-layouts  8.17 us (5%)
    pallas_call x1, Pallas kernels, local(): pl.pallas_call(kernel, out_shape=(outs, outs), in_specs=[hbm, hbm, hbm, p...  155 us
    unnamed x16, local copies, waits for them, and re-layouts  8.17 us

commit v1 on v0

--- a/solution.py
+++ b/solution.py
@@ -19,6 +19,9 @@
 COLS = 512
 OBS_SUB = 128
 TALL = ROWS + 2 * STEPS
+AHEAD = 4
+FIRST = 15
+SHARES = (15, 20, 26, 30)
 MESH = pl.DeviceIdType.MESH
 F32 = jnp.float32
 
@@ -44,20 +47,14 @@
     return wide[:, :width] + wide[:, width:]
 
 
-def forecast_rows(field, pace, step, low, high, unroll):
+def forecast_rows(field, pace, step, low, high):
     source, target = (step + 1) % 2, step % 2
-    lane = lax.broadcasted_iota(jnp.int32, (OWN, COLS), 1)
-
-    def one(row, held):
-        above, here = held
-        below = field[source, row + 1]
-        west = jnp.where(lane == 0, 0.0, pltpu.roll(here, 1, 1))
-        east = jnp.where(lane == COLS - 1, 0.0, pltpu.roll(here, COLS - 1, 1))
-        spread = below + above + east + west - 4.0 * here
-        field[target, row] = 2.0 * here - field[target, row] + pace[row] * spread
-        return here, below
-
-    lax.fori_loop(low, high, one, (field[source, low - 1], field[source, low]), unroll=unroll)
+    lane = lax.broadcasted_iota(jnp.int32, (high - low, OWN, COLS), 2)
+    here = field[source, low:high]
+    west = jnp.where(lane == 0, 0.0, pltpu.roll(here, 1, 2))
+    east = jnp.where(lane == COLS - 1, 0.0, pltpu.roll(here, COLS - 1, 2))
+    spread = field[source, low + 1 : high + 1] + field[source, low - 1 : high - 1] + east + west - 4.0 * here
+    return 2.0 * here - field[target, low:high] + pace[low:high] * spread
 
 
 def kernel(
@@ -125,6 +122,23 @@
     for load in loads:
         load.wait()
 
+    def turn(group, _):
+        at = pl.multiple_of(group * 8, 8)
+        for index in range(2):
+            field[index, pl.ds(at + STEPS, 8)] = jnp.transpose(raw[index, :, pl.ds(at, 8), :], (1, 0, 2))
+        rows = pace_raw[pl.ds(at, 8), :]
+        pace[pl.ds(at + STEPS, 8)] = jnp.broadcast_to(rows[:, None, :], (8, OWN, COLS))
+        return 0
+
+    lax.fori_loop(0, ROWS // 8, turn, 0)
+
+    def inner(step):
+        low, high = STEPS + step, STEPS + ROWS - step
+        field[step % 2, low:high] = forecast_rows(field, pace, step, low, high)
+
+    for step in range(1, AHEAD + 1):
+        inner(step)
+
     pl.semaphore_wait(barrier, GROUP - 1 + 7)
 
     rims = []
@@ -153,25 +167,21 @@
     for copy in rims:
         copy.start()
 
-    def turn(group, _):
-        at = pl.multiple_of(group * 8, 8)
-        for index in range(2):
-            field[index, pl.ds(at + STEPS, 8)] = jnp.transpose(raw[index, :, pl.ds(at, 8), :], (1, 0, 2))
-        rows = pace_raw[pl.ds(at, 8), :]
-        pace[pl.ds(at + STEPS, 8)] = jnp.broadcast_to(rows[:, None, :], (8, OWN, COLS))
-        return 0
-
-    lax.fori_loop(0, ROWS // 8, turn, 0)
-
-    for step in range(1, STEPS + 1):
-        forecast_rows(field, pace, step, STEPS + step, STEPS + ROWS - step, 2)
-
-    def ship(part, edges):
-        def one(step, _):
+    for step in range(AHEAD + 1, STEPS + 1):
+        inner(step)
+
+
+    def ship(first, last, early):
+        def one(number, _):
+            part = lax.div(number, GROUP - 1)
+            step = lax.rem(number, GROUP - 1) + 1
             peer = lax.rem(mem + step, GROUP)
-            outer = jnp.logical_or(peer < 2, peer > GROUP - 3)
-
-            def go():
+            ahead = jnp.logical_and(
+                jnp.logical_and(peer >= 2, peer < GROUP - 2), jnp.logical_and(part == 0, step <= FIRST)
+            )
+
+            @pl.when(ahead if early else jnp.logical_not(ahead))
+            def _():
                 pltpu.make_async_remote_copy(
                     src_ref=field.at[:, STEPS + STRIP * peer + part],
                     dst_ref=arrived.at[part, mem],
@@ -181,15 +191,12 @@
                     device_id_type=MESH,
                 ).start()
 
-            if edges is None:
-                go()
-            else:
-                pl.when(outer if edges else jnp.logical_not(outer))(go)
             return 0
 
-        lax.fori_loop(1, GROUP, one, 0)
-
-    ship(0, False)
+        lax.fori_loop(first, last, one, 0)
+
+    if FIRST:
+        ship(0, FIRST, True)
 
     for copy in rims:
         copy.wait_recv()
@@ -200,8 +207,12 @@
         rows = pace_rim[side_index] * keep
         pace[at : at + STEPS] = jnp.broadcast_to(rows[:, None, :], (STEPS, OWN, COLS))
     for step in range(1, STEPS + 1):
-        forecast_rows(field, pace, step, step, STEPS + step, 2)
-        forecast_rows(field, pace, step, STEPS + ROWS - step, ROWS + 2 * STEPS - step, 2)
+        tops = step, STEPS + step
+        ends = STEPS + ROWS - step, TALL - step
+        upper = forecast_rows(field, pace, step, *tops)
+        lower = forecast_rows(field, pace, step, *ends)
+        field[step % 2, tops[0] : tops[1]] = upper
+        field[step % 2, ends[0] : ends[1]] = lower
 
     lane_all = lax.broadcasted_iota(jnp.int32, (OWN, COLS), 1)
     lane = lax.broadcasted_iota(jnp.int32, (OWN, OBS_SUB), 1)
@@ -230,9 +241,7 @@
 
     lax.fori_loop(1, GROUP, tell, 0)
 
-    ship(0, True)
-    for part in range(1, STRIP):
-        ship(part, None)
+    ship(0, SHARES[0], False)
     for part in range(STRIP):
         arrived[part, mem] = field[:, STEPS + STRIP * mem + part]
 
@@ -256,13 +265,18 @@
     crossing = pass_on(own, across, 1)
     for other in tiers:
         pass_on(own, other, 2)
+    ship(SHARES[0], SHARES[1], False)
     crossing.wait_recv()
     for other in tiers:
         pass_on(met, other, 3)
+    ship(SHARES[1], SHARES[2], False)
     third = seen.at[0, pl.ds(0, 3), 0]
     pltpu.make_async_copy(third, third, obs_recv.at[2]).wait()
     pltpu.make_async_copy(third, third, obs_recv.at[3]).wait()
-    pass_on(seen.at[core], twin, 4).wait_recv()
+    swap = pass_on(seen.at[core], twin, 4)
+    ship(SHARES[2], SHARES[3], False)
+    swap.wait_recv()
+    ship(SHARES[3], STRIP * (GROUP - 1), False)
 
     blocks = taper_ref.shape[0]
     lines = blocks * ENS
@@ -420,7 +434,7 @@
             pltpu.SemaphoreType.DMA,
         ],
         compiler_params=pltpu.CompilerParams(
-            collective_id=0, has_side_effects=True, vmem_limit_bytes=48 * 2**20
+            collective_id=0, has_side_effects=True, vmem_limit_bytes=60 * 2**20
         ),
     )(
         now_field,

time: 165 us -> 125 us (0.76)
  Pallas kernels: 155 us -> 121 us
  local copies, waits for them, and re-layouts: 8.17 us -> 3.32 us
    pallas_call x1, Pallas kernels: 155 us -> 121 us  [local(): pl.pallas_call(kernel, out_shape=(outs, outs), in_specs=[hbm, hbm, hbm, p...]
    unnamed x16 -> x4, local copies, waits for them, and re-layouts: 8.17 us -> 3.32 us
where the time goes in v1:
time: 125 us
  Pallas kernels  121 us (97%)
  local copies, waits for them, and re-layouts  3.32 us (3%)
    pallas_call x1, Pallas kernels, local(): pl.pallas_call(kernel, out_shape=(outs, outs), in_specs=[hbm, hbm, hbm, p...  121 us
    unnamed x4, local copies, waits for them, and re-layouts  3.32 us

profile of v1, /device:TPU:1, one launch (start us, length us, event | category | flops | bytes accessed | tf_op | source)
XLA Modules:
  0.0 124.8 jit_solution(11026972206678741249)
XLA Ops:
  0.6 120.8 %shard_map.86 = (f32[8,64,512]{2,1,0:T(8,128)}, f32[8,64,512]{2,1,0:T(8,128)}) custom-call(f32[8,64,512]{2,1,0:T(8,128)} %now_hbm.1, f32[8,64,512]{2,1,0:T(8,128)} %prev_hbm.1, f32[64,512]{1,0:T(8,128)} %speed_hbm.1, s32[128]{0:T(128)} %cells_ref.1, f32[1,2048]{1,0:T(1,128)} %bitcast.2, f32[1,2048]{1,0:T(1,128)} %bitcast.3, f32[8,2048]{1,0:T(8,128)} %taper_ref.1), custom_call_target="tpu_custom_call" | custom-call | tf_op jit(solution)/shard_map/pallas_call | solution.py:407
  121.4 0.0 copy-start
  121.4 2.4 %copy.11 = f32[8,64,512]{2,1,0:T(8,128)} copy(f32[8,64,512]{2,1,0:T(8,128)} %get-tuple-element.4) | data formatting | bytes 2097152
  123.8 0.0 copy-done
  123.8 1.0 copy.12
Async XLA Ops:
  121.4 2.4 %copy-start = (f32[8,64,512]{2,1,0:T(8,128)S(1)}, f32[8,64,512]{2,1,0:T(8,128)}, u32[]{:S(2)}) copy-start(f32[8,64,512]{2,1,0:T(8,128)} %get-tuple-element.5) | copy-start | bytes 3145732

commit v2 on v1

--- a/solution.py
+++ b/solution.py
@@ -17,9 +17,13 @@
 ROWS = 64
 STRIP = 4
 COLS = 512
+CHUNK = 16
 OBS_SUB = 128
 TALL = ROWS + 2 * STEPS
-AHEAD = 4
+AHEAD = -1
+MARGIN = 8
+SHY = (STEPS + MARGIN) // STRIP
+EARLY = 1
 FIRST = 15
 SHARES = (15, 20, 26, 30)
 MESH = pl.DeviceIdType.MESH
@@ -65,8 +69,7 @@
     values_ref,
     precision_ref,
     taper_ref,
-    now_out,
-    prev_out,
+    settled,
     raw,
     rim,
     pace_raw,
@@ -79,7 +82,6 @@
     root,
     arrived,
     leaving,
-    settled,
     load_sem,
     rim_send,
     rim_recv,
@@ -89,6 +91,7 @@
     out_recv,
     back_send,
     back_recv,
+    keep_sem,
 ):
     mem, sub = lax.axis_index("mem"), lax.axis_index("sub")
     core = lax.rem(sub, 2)
@@ -112,6 +115,36 @@
 
     lax.fori_loop(1, GROUP, greet, 0)
 
+    def meet():
+        pl.semaphore_wait(barrier, GROUP - 1 + 7)
+
+        rims = []
+        for side_index, (other, first) in enumerate(((below, ROWS - STEPS), (above, 0))):
+            for index, source in enumerate((now_hbm, prev_hbm)):
+                rims.append(
+                    pltpu.make_async_remote_copy(
+                        src_ref=source.at[:, first : first + STEPS, :],
+                        dst_ref=rim.at[side_index, index],
+                        send_sem=rim_send.at[side_index, index],
+                        recv_sem=rim_recv.at[side_index, index],
+                        device_id={"sub": other},
+                        device_id_type=MESH,
+                    )
+                )
+            rims.append(
+                pltpu.make_async_remote_copy(
+                    src_ref=speed_hbm.at[first : first + STEPS, :],
+                    dst_ref=pace_rim.at[side_index],
+                    send_sem=rim_send.at[side_index, 2],
+                    recv_sem=rim_recv.at[side_index, 2],
+                    device_id={"sub": other},
+                    device_id_type=MESH,
+                )
+            )
+        for copy in rims:
+            copy.start()
+        return rims
+
     loads = [
         pltpu.make_async_copy(now_hbm, raw.at[0], load_sem.at[0]),
         pltpu.make_async_copy(prev_hbm, raw.at[1], load_sem.at[1]),
@@ -119,6 +152,8 @@
     ]
     for load in loads:
         load.start()
+    if AHEAD < 0:
+        rims = meet()
     for load in loads:
         load.wait()
 
@@ -133,41 +168,15 @@
     lax.fori_loop(0, ROWS // 8, turn, 0)
 
     def inner(step):
-        low, high = STEPS + step, STEPS + ROWS - step
+        low, high = STEPS + MARGIN + step, STEPS + ROWS - MARGIN - step
         field[step % 2, low:high] = forecast_rows(field, pace, step, low, high)
 
     for step in range(1, AHEAD + 1):
         inner(step)
 
-    pl.semaphore_wait(barrier, GROUP - 1 + 7)
-
-    rims = []
-    for side_index, (other, first) in enumerate(((below, ROWS - STEPS), (above, 0))):
-        for index, source in enumerate((raw.at[0], raw.at[1])):
-            rims.append(
-                pltpu.make_async_remote_copy(
-                    src_ref=source.at[:, first : first + STEPS, :],
-                    dst_ref=rim.at[side_index, index],
-                    send_sem=rim_send.at[side_index, index],
-                    recv_sem=rim_recv.at[side_index, index],
-                    device_id={"sub": other},
-                    device_id_type=MESH,
-                )
-            )
-        rims.append(
-            pltpu.make_async_remote_copy(
-                src_ref=pace_raw.at[first : first + STEPS, :],
-                dst_ref=pace_rim.at[side_index],
-                send_sem=rim_send.at[side_index, 2],
-                recv_sem=rim_recv.at[side_index, 2],
-                device_id={"sub": other},
-                device_id_type=MESH,
-            )
-        )
-    for copy in rims:
-        copy.start()
-
-    for step in range(AHEAD + 1, STEPS + 1):
+    if AHEAD >= 0:
+        rims = meet()
+    for step in range(max(AHEAD, 0) + 1, STEPS + 1):
         inner(step)
 
 
@@ -177,7 +186,7 @@
             step = lax.rem(number, GROUP - 1) + 1
             peer = lax.rem(mem + step, GROUP)
             ahead = jnp.logical_and(
-                jnp.logical_and(peer >= 2, peer < GROUP - 2), jnp.logical_and(part == 0, step <= FIRST)
+                jnp.logical_and(peer >= SHY, peer < GROUP - SHY), jnp.logical_and(part < EARLY, step <= FIRST)
             )
 
             @pl.when(ahead if early else jnp.logical_not(ahead))
@@ -196,7 +205,7 @@
         lax.fori_loop(first, last, one, 0)
 
     if FIRST:
-        ship(0, FIRST, True)
+        ship(0, EARLY * (GROUP - 1), True)
 
     for copy in rims:
         copy.wait_recv()
@@ -207,8 +216,8 @@
         rows = pace_rim[side_index] * keep
         pace[at : at + STEPS] = jnp.broadcast_to(rows[:, None, :], (STEPS, OWN, COLS))
     for step in range(1, STEPS + 1):
-        tops = step, STEPS + step
-        ends = STEPS + ROWS - step, TALL - step
+        tops = step, STEPS + MARGIN + step
+        ends = STEPS + ROWS - MARGIN - step, TALL - step
         upper = forecast_rows(field, pace, step, *tops)
         lower = forecast_rows(field, pace, step, *ends)
         field[step % 2, tops[0] : tops[1]] = upper
@@ -343,6 +352,11 @@
         shift = product(side(product(side(pulled), right)), right)
         iterate[b] = math.sqrt(ENS - 1.0) * final + shift[0:1]
 
+    def keep_own(part):
+        return pltpu.make_async_copy(
+            leaving.at[part, mem], settled.at[:, STRIP * mem + part], keep_sem.at[part]
+        )
+
     def settle(part):
         for half in range(COLS // BLOCK):
             mixing = side(iterate[2 * part + half])
@@ -370,7 +384,7 @@
             return 0
 
         lax.fori_loop(1, GROUP, back, 0)
-        settled[:, STRIP * mem + part] = leaving[part, mem]
+        keep_own(part).start()
 
     for part in range(STRIP):
         strip = arrived.at[0, pl.ds(0, GROUP - 1)]
@@ -380,14 +394,8 @@
     everything = arrived.at[:, pl.ds(0, GROUP - 1)]
     pltpu.make_async_copy(everything, everything, back_recv).wait()
 
-    def finish(group, _):
-        at = pl.multiple_of(group * 8, 8)
-        for index, out in enumerate((now_out, prev_out)):
-            out[:, pl.ds(at, 8), :] = jnp.transpose(settled[index, pl.ds(at, 8)], (1, 0, 2))
-        return 0
-
-    lax.fori_loop(0, ROWS // 8, finish, 0)
-
+    for part in range(STRIP):
+        keep_own(part).wait()
     for copy in rims:
         copy.wait_send()
     pltpu.make_async_copy(whole, whole, obs_send.at[0]).wait()
@@ -399,16 +407,38 @@
     pltpu.make_async_copy(everything, everything, back_send).wait()
 
 
+def turn_back(settled_hbm, now_hbm, prev_hbm, rows, turned, load_sem, store_sem):
+    places = [(index, slice(at, at + CHUNK)) for index in range(2) for at in range(0, ROWS, CHUNK)]
+
+    def load(number):
+        index, at = places[number]
+        return pltpu.make_async_copy(settled_hbm.at[index, at], rows.at[index, at], load_sem.at[number])
+
+    def store(number):
+        index, at = places[number]
+        out = (now_hbm, prev_hbm)[index]
+        return pltpu.make_async_copy(turned.at[index, :, at], out.at[:, at], store_sem.at[number])
+
+    for number in range(len(places)):
+        load(number).start()
+    for number, (index, at) in enumerate(places):
+        load(number).wait()
+        turned[index, :, at] = jnp.transpose(rows[index, at], (1, 0, 2))
+        store(number).start()
+    for number in range(len(places)):
+        store(number).wait()
+
+
 def local(now_field, prev_field, speed, obs_cells, obs_values, obs_precision, taper):
     blocks = taper.shape[0]
-    hbm = pl.BlockSpec(memory_space=pl.ANY)
+    hbm = pl.BlockSpec(memory_space=pltpu.HBM)
     vmem = pl.BlockSpec(memory_space=pltpu.VMEM)
     outs = jax.ShapeDtypeStruct((OWN, ROWS, COLS), F32)
-    return pl.pallas_call(
+    settled = pl.pallas_call(
         kernel,
-        out_shape=(outs, outs),
+        out_shape=jax.ShapeDtypeStruct((2, ROWS, OWN, COLS), F32),
         in_specs=[hbm, hbm, hbm, pl.BlockSpec(memory_space=pltpu.SMEM), vmem, vmem, vmem],
-        out_specs=(vmem, vmem),
+        out_specs=hbm,
         scratch_shapes=[
             pltpu.VMEM((2, OWN, ROWS, COLS), F32),
             pltpu.VMEM((2, 2, OWN, STEPS, COLS), F32),
@@ -422,7 +452,6 @@
             pltpu.VMEM((blocks, ENS, ENS), F32),
             pltpu.VMEM((STRIP, GROUP, 2, OWN, COLS), F32),
             pltpu.VMEM((STRIP, GROUP, 2, OWN, COLS), F32),
-            pltpu.VMEM((2, ROWS, OWN, COLS), F32),
             pltpu.SemaphoreType.DMA((3,)),
             pltpu.SemaphoreType.DMA((2, 3)),
             pltpu.SemaphoreType.DMA((2, 3)),
@@ -432,6 +461,7 @@
             pltpu.SemaphoreType.DMA((STRIP,)),
             pltpu.SemaphoreType.DMA,
             pltpu.SemaphoreType.DMA,
+            pltpu.SemaphoreType.DMA((STRIP,)),
         ],
         compiler_params=pltpu.CompilerParams(
             collective_id=0, has_side_effects=True, vmem_limit_bytes=60 * 2**20
@@ -445,6 +475,20 @@
         obs_precision[None, :],
         taper,
     )
+    copies = 2 * ROWS // CHUNK
+    return pl.pallas_call(
+        turn_back,
+        out_shape=(outs, outs),
+        in_specs=[hbm],
+        out_specs=(hbm, hbm),
+        scratch_shapes=[
+            pltpu.VMEM((2, ROWS, OWN, COLS), F32),
+            pltpu.VMEM((2, OWN, ROWS, COLS), F32),
+            pltpu.SemaphoreType.DMA((copies,)),
+            pltpu.SemaphoreType.DMA((copies,)),
+        ],
+        compiler_params=pltpu.CompilerParams(vmem_limit_bytes=60 * 2**20),
+    )(settled)
 
 
 def solution(mesh):

time: 125 us -> 122 us (0.976); the launches traced: 125 us -> 120 us
  local copies, waits for them, and re-layouts: 3.32 us -> 0 us
  Pallas kernels: 121 us -> 119 us
    unnamed x4 -> x0, local copies, waits for them, and re-layouts: 3.32 us -> none
    pallas_call x1 -> x2, Pallas kernels: 121 us -> 119 us  [the longest x1 117 us: local(): pl.pallas_call(kernel, out_shape=jax.ShapeDtypeStruct((2, ROWS, OWN, COLS...]
where the time goes in v2:
time: 122 us; the launch traced here: 120 us
  Pallas kernels  119 us (98%)
    pallas_call x1, Pallas kernels, local(): pl.pallas_call(kernel, out_shape=jax.ShapeDtypeStruct((2, ROWS, OWN, COLS...  117 us
    pallas_call x1, Pallas kernels, local(): pl.pallas_call(turn_back, out_shape=(outs, outs), in_specs=[hbm], out_spe...  2.44 us

profile of v2, /device:TPU:1, one launch (start us, length us, event | category | flops | bytes accessed | tf_op | source)
XLA Modules:
  0.0 119.7 jit_solution(16884119247049428071)
XLA Ops:
  0.6 116.6 %shard_map.86.settled_hbm = f32[2,64,8,512]{3,2,1,0:T(8,128)} custom-call(f32[8,64,512]{2,1,0:T(8,128)} %now_hbm.1, f32[8,64,512]{2,1,0:T(8,128)} %prev_hbm.1, f32[64,512]{1,0:T(8,128)} %speed_hbm.1, s32[128]{0:T(128)} %cells_ref.1, f32[1,2048]{1,0:T(1,128)} %bitcast.2, f32[1,2048]{1,0:T(1,128)} %bitcast.3, f32[8,2048]{1,0:T(8,128)} %taper_ref.1), custom_call_target="tpu_custom_call" | custom-call | tf_op jit(solution)/shard_map/pallas_call | solution.py:437
  117.3 2.4 %shard_map.87 = (f32[8,64,512]{2,1,0:T(8,128)}, f32[8,64,512]{2,1,0:T(8,128)}) custom-call(f32[2,64,8,512]{3,2,1,0:T(8,128)} %shard_map.86.settled_hbm), custom_call_target="tpu_custom_call" | custom-call | tf_op jit(solution)/shard_map/pallas_call | solution.py:479

commit v3 on v2

--- a/solution.py
+++ b/solution.py
@@ -21,11 +21,11 @@
 OBS_SUB = 128
 TALL = ROWS + 2 * STEPS
 AHEAD = -1
-MARGIN = 8
+MARGIN = 4
 SHY = (STEPS + MARGIN) // STRIP
 EARLY = 1
 FIRST = 15
-SHARES = (15, 20, 26, 30)
+SHARES = (15, 24, 34, 44)
 MESH = pl.DeviceIdType.MESH
 F32 = jnp.float32
 
@@ -330,8 +330,10 @@
         full = wide[:, :ENS] + wide[:, ENS:] + (ENS - 1.0) * eye
         scale = jnp.sum(jnp.sum(full * eye, axis=1, keepdims=True), axis=0, keepdims=True)
         scales.append(scale)
-        iterate[b] = full / scale
-        root[b] = eye
+        start = full / scale
+        factor = 1.5 * eye - 0.5 * start
+        iterate[b] = product(side(start), tile(factor))
+        root[b] = factor
 
     def sweep(_, carry):
         for b in range(blocks):
@@ -341,10 +343,11 @@
             root[b] = product(side(factor), tile(base))
         return carry
 
-    lax.fori_loop(0, NS_ITERS, sweep, 0)
+    lax.fori_loop(1, NS_ITERS - 1, sweep, 0)
 
     for b in range(blocks):
-        final = root[b] / jnp.sqrt(scales[b])
+        factor = 1.5 * eye - 0.5 * product(side(root[b]), tile(iterate[b]))
+        final = product(side(factor), tile(root[b])) / jnp.sqrt(scales[b])
         wide = gram[lines : lines + 8, :]
         pulled = (wide[:, :ENS] + wide[:, ENS:])[b : b + 1]
         pulled = jnp.broadcast_to(pulled, (16, ENS))

time: 122 us -> 121 us (level); the launches traced: 120 us -> 121 us
  no operation moved by 1% of the time
where the time goes in v3:
time: 121 us
  Pallas kernels  120 us (99%)
    pallas_call x1, Pallas kernels, local(): pl.pallas_call(kernel, out_shape=jax.ShapeDtypeStruct((2, ROWS, OWN, COLS...  118 us
    pallas_call x1, Pallas kernels, local(): pl.pallas_call(turn_back, out_shape=(outs, outs), in_specs=[hbm], out_spe...  2.44 us

profile of v3, /device:TPU:1, one launch (start us, length us, event | category | flops | bytes accessed | tf_op | source)
XLA Modules:
  0.0 120.7 jit_solution(18221400964425428041)
XLA Ops:
  0.6 117.7 %shard_map.86.settled_hbm = f32[2,64,8,512]{3,2,1,0:T(8,128)} custom-call(f32[8,64,512]{2,1,0:T(8,128)} %now_hbm.1, f32[8,64,512]{2,1,0:T(8,128)} %prev_hbm.1, f32[64,512]{1,0:T(8,128)} %speed_hbm.1, s32[128]{0:T(128)} %cells_ref.1, f32[1,2048]{1,0:T(1,128)} %bitcast.2, f32[1,2048]{1,0:T(1,128)} %bitcast.3, f32[8,2048]{1,0:T(8,128)} %taper_ref.1), custom_call_target="tpu_custom_call" | custom-call | tf_op jit(solution)/shard_map/pallas_call | solution.py:440
  118.3 2.4 %shard_map.87 = (f32[8,64,512]{2,1,0:T(8,128)}, f32[8,64,512]{2,1,0:T(8,128)}) custom-call(f32[2,64,8,512]{3,2,1,0:T(8,128)} %shard_map.86.settled_hbm), custom_call_target="tpu_custom_call" | custom-call | tf_op jit(solution)/shard_map/pallas_call | solution.py:482

commit v4 on v3

--- a/solution.py
+++ b/solution.py
@@ -51,14 +51,14 @@
     return wide[:, :width] + wide[:, width:]
 
 
-def forecast_rows(field, pace, step, low, high):
+def forecast_rows(field, pace, keep, step, low, high):
     source, target = (step + 1) % 2, step % 2
     lane = lax.broadcasted_iota(jnp.int32, (high - low, OWN, COLS), 2)
     here = field[source, low:high]
     west = jnp.where(lane == 0, 0.0, pltpu.roll(here, 1, 2))
     east = jnp.where(lane == COLS - 1, 0.0, pltpu.roll(here, COLS - 1, 2))
-    spread = field[source, low + 1 : high + 1] + field[source, low - 1 : high - 1] + east + west - 4.0 * here
-    return 2.0 * here - field[target, low:high] + pace[low:high] * spread
+    beside = field[source, low + 1 : high + 1] + field[source, low - 1 : high - 1] + east + west
+    return keep[low:high] * here - field[target, low:high] + pace[low:high] * beside
 
 
 def kernel(
@@ -75,6 +75,7 @@
     pace_raw,
     pace_rim,
     pace,
+    hold,
     field,
     seen,
     gram,
@@ -163,13 +164,14 @@
             field[index, pl.ds(at + STEPS, 8)] = jnp.transpose(raw[index, :, pl.ds(at, 8), :], (1, 0, 2))
         rows = pace_raw[pl.ds(at, 8), :]
         pace[pl.ds(at + STEPS, 8)] = jnp.broadcast_to(rows[:, None, :], (8, OWN, COLS))
+        hold[pl.ds(at + STEPS, 8)] = jnp.broadcast_to((2.0 - 4.0 * rows)[:, None, :], (8, OWN, COLS))
         return 0
 
     lax.fori_loop(0, ROWS // 8, turn, 0)
 
     def inner(step):
         low, high = STEPS + MARGIN + step, STEPS + ROWS - MARGIN - step
-        field[step % 2, low:high] = forecast_rows(field, pace, step, low, high)
+        field[step % 2, low:high] = forecast_rows(field, pace, hold, step, low, high)
 
     for step in range(1, AHEAD + 1):
         inner(step)
@@ -215,11 +217,12 @@
             field[index, at : at + STEPS] = jnp.transpose(rim[side_index, index], (1, 0, 2)) * keep
         rows = pace_rim[side_index] * keep
         pace[at : at + STEPS] = jnp.broadcast_to(rows[:, None, :], (STEPS, OWN, COLS))
+        hold[at : at + STEPS] = jnp.broadcast_to((2.0 - 4.0 * rows)[:, None, :], (STEPS, OWN, COLS))
     for step in range(1, STEPS + 1):
         tops = step, STEPS + MARGIN + step
         ends = STEPS + ROWS - MARGIN - step, TALL - step
-        upper = forecast_rows(field, pace, step, *tops)
-        lower = forecast_rows(field, pace, step, *ends)
+        upper = forecast_rows(field, pace, hold, step, *tops)
+        lower = forecast_rows(field, pace, hold, step, *ends)
         field[step % 2, tops[0] : tops[1]] = upper
         field[step % 2, ends[0] : ends[1]] = lower
 
@@ -447,6 +450,7 @@
             pltpu.VMEM((2, 2, OWN, STEPS, COLS), F32),
             pltpu.VMEM((ROWS, COLS), F32),
             pltpu.VMEM((2, STEPS, COLS), F32),
+            pltpu.VMEM((TALL, OWN, COLS), F32),
             pltpu.VMEM((TALL, OWN, COLS), F32),
             pltpu.VMEM((2, TALL, OWN, COLS), F32),
             pltpu.VMEM((2, 4, 2, GROUP, OWN, OBS_SUB), F32),

time: 121 us -> 119 us (0.983)
    pallas_call x1, Pallas kernels: 118 us -> 116 us  [local(): pl.pallas_call(kernel, out_shape=jax.ShapeDtypeStruct((2, ROWS, OWN, COLS...]
where the time goes in v4:
time: 119 us
  Pallas kernels  119 us (100%)
    pallas_call x1, Pallas kernels, local(): pl.pallas_call(kernel, out_shape=jax.ShapeDtypeStruct((2, ROWS, OWN, COLS...  116 us
    pallas_call x1, Pallas kernels, local(): pl.pallas_call(turn_back, out_shape=(outs, outs), in_specs=[hbm], out_spe...  2.44 us

profile of v4, /device:TPU:1, one launch (start us, length us, event | category | flops | bytes accessed | tf_op | source)
XLA Modules:
  0.0 119.3 jit_solution(4792716728865730775)
XLA Ops:
  0.6 116.2 %shard_map.86.settled_hbm = f32[2,64,8,512]{3,2,1,0:T(8,128)} custom-call(f32[8,64,512]{2,1,0:T(8,128)} %now_hbm.1, f32[8,64,512]{2,1,0:T(8,128)} %prev_hbm.1, f32[64,512]{1,0:T(8,128)} %speed_hbm.1, s32[128]{0:T(128)} %cells_ref.1, f32[1,2048]{1,0:T(1,128)} %bitcast.2, f32[1,2048]{1,0:T(1,128)} %bitcast.3, f32[8,2048]{1,0:T(8,128)} %taper_ref.1), custom_call_target="tpu_custom_call" | custom-call | tf_op jit(solution)/shard_map/pallas_call | solution.py:443
  116.9 2.4 %shard_map.87 = (f32[8,64,512]{2,1,0:T(8,128)}, f32[8,64,512]{2,1,0:T(8,128)}) custom-call(f32[2,64,8,512]{3,2,1,0:T(8,128)} %shard_map.86.settled_hbm), custom_call_target="tpu_custom_call" | custom-call | tf_op jit(solution)/shard_map/pallas_call | solution.py:486

commit v5 on v4

--- a/solution.py
+++ b/solution.py
@@ -25,7 +25,7 @@
 SHY = (STEPS + MARGIN) // STRIP
 EARLY = 1
 FIRST = 15
-SHARES = (15, 24, 34, 44)
+SHARES = (18, 28, 40, 50)
 MESH = pl.DeviceIdType.MESH
 F32 = jnp.float32
 

time: 119 us -> 118 us (level)
  Pallas kernels: 119 us -> 117 us
    pallas_call x1, Pallas kernels: 116 us -> 114 us  [local(): pl.pallas_call(kernel, out_shape=jax.ShapeDtypeStruct((2, ROWS, OWN, COLS...]
where the time goes in v5:
time: 118 us; the launch traced here: 117 us
  Pallas kernels  117 us (99%)
    pallas_call x1, Pallas kernels, local(): pl.pallas_call(kernel, out_shape=jax.ShapeDtypeStruct((2, ROWS, OWN, COLS...  114 us
    pallas_call x1, Pallas kernels, local(): pl.pallas_call(turn_back, out_shape=(outs, outs), in_specs=[hbm], out_spe...  2.44 us

profile of v5, /device:TPU:1, one launch (start us, length us, event | category | flops | bytes accessed | tf_op | source)
XLA Modules:
  0.0 117.3 jit_solution(16091678775957351800)
XLA Ops:
  0.6 114.2 %shard_map.86.settled_hbm = f32[2,64,8,512]{3,2,1,0:T(8,128)} custom-call(f32[8,64,512]{2,1,0:T(8,128)} %now_hbm.1, f32[8,64,512]{2,1,0:T(8,128)} %prev_hbm.1, f32[64,512]{1,0:T(8,128)} %speed_hbm.1, s32[128]{0:T(128)} %cells_ref.1, f32[1,2048]{1,0:T(1,128)} %bitcast.2, f32[1,2048]{1,0:T(1,128)} %bitcast.3, f32[8,2048]{1,0:T(8,128)} %taper_ref.1), custom_call_target="tpu_custom_call" | custom-call | tf_op jit(solution)/shard_map/pallas_call | solution.py:443
  114.9 2.4 %shard_map.87 = (f32[8,64,512]{2,1,0:T(8,128)}, f32[8,64,512]{2,1,0:T(8,128)}) custom-call(f32[2,64,8,512]{3,2,1,0:T(8,128)} %shard_map.86.settled_hbm), custom_call_target="tpu_custom_call" | custom-call | tf_op jit(solution)/shard_map/pallas_call | solution.py:486
